TPU v7x, 32 devices: a whole 2x2x4 slice. The times are simulated.
32 devices in a mesh: streams: 2 (over y), span: 4 (over z), head: 2 (over x), seq: 2 (over core).
Axes of the slice: x: 2, y: 2, z: 4, core: 2. Of those that a mesh axis runs over, the one named last changes fastest.
Arguments:
- query_rows: bfloat16 [4096, 1280], P(('streams', 'span', 'seq'), 'head'), parts along dimension 0, may hold values from -100 to 100
- key_rows: bfloat16 [4096, 1280], P(('streams', 'span', 'seq'), 'head'), parts along dimension 0, may hold values from -5 to 5
- value_rows: bfloat16 [4096, 1280], P(('streams', 'span', 'seq'), 'head'), parts along dimension 0, may hold values from -6 to 6
- out_weight: bfloat16 [1280, 5120], P('head', 'seq'), may hold values from -0.59765625 to 0.59765625
- gate_table: float32 [4, 5120], P(None, 'head'), may hold values from 0.5 to 2
- step_index: int32 [8], P('streams'), parts along dimension 0, may hold values from 0 to 3
- block_mask: int32 [8, 4], P('streams'), parts along dimension 0, may hold values from 0 to 1, as said below
Outputs:
- gated_update: bfloat16 [4096, 5120], P(('streams', 'span', 'seq'), 'head'), parts along dimension 0
There are 2 independent parts, one for each index of `streams`. A program takes and returns all parts, laid end to end along the dimension named above; an argument that names none is the same for every part. Nothing has to cross between parts.
Inputs may be any that keep to these rules, and one draw needn't show every extreme that they name: block_mask[c, c] = 1 and block_mask[c, e] = 0 for e > c; entries below the diagonal are 0 or 1.
All inputs are finite; a program needn't handle non-finite values.
Results may differ from a plain program's by a relative error of at most 0.017.
Values may be sent and summed in bfloat16 or wider, within the bound.
No kernel may reach another device: no remote copies, remote signals or barrier semaphores. Data moves between devices by JAX's collectives and lax.ppermute only.
A program may use at most 192 MiB of HBM per device.

v0:
```python
import math
import jax
import jax.numpy as jnp
from jax import lax
from jax.sharding import PartitionSpec as P

HD = 128
NEG_FLOOR = -1e30


def on_device(query_rows, key_rows, value_rows, out_weight, gate_table, step_index, block_mask):
    tok_rows = query_rows.shape[0]
    heads_here = query_rows.shape[1] // HD
    group_count = lax.axis_size("span")
    span_tok = tok_rows * lax.axis_size("seq")
    my_span = lax.axis_index("span")
    group_ids = jnp.arange(group_count, dtype=jnp.int32)
    mask_row = jnp.sum(jnp.where(group_ids[:, None] == my_span, block_mask, 0), axis=0)
    query_three = query_rows.reshape(tok_rows, heads_here, HD)
    score_scale = 1.0 / math.sqrt(HD)
    run_max = jnp.full((heads_here, tok_rows), NEG_FLOOR, jnp.float32)
    key_part = lax.all_gather(key_rows, ("span", "seq"), axis=0, tiled=True)
    value_part = lax.all_gather(value_rows, ("span", "seq"), axis=0, tiled=True)
    piece_rows = key_part.shape[0]
    key_group = jnp.arange(piece_rows, dtype=jnp.int32) // span_tok
    visible = (
        jnp.sum(jnp.where(key_group[:, None] == group_ids[None, :], mask_row[None, :], 0), axis=1)
        == 1
    )
    scores = (
        jnp.einsum(
            "thd,khd->htk",
            query_three,
            key_part.reshape(piece_rows, heads_here, HD),
            preferred_element_type=jnp.float32,
        )
        * score_scale
    )
    scores = jnp.where(visible[None, None, :], scores, NEG_FLOOR)
    new_max = jnp.maximum(run_max, jnp.max(scores, axis=2))
    probs = jnp.where(visible[None, None, :], jnp.exp(scores - new_max[:, :, None]), 0.0)
    run_total = jnp.sum(probs, axis=2)
    added = jnp.einsum(
        "htk,khd->htd",
        probs.astype(jnp.bfloat16),
        value_part.reshape(piece_rows, heads_here, HD),
        preferred_element_type=jnp.float32,
    )
    run_accum = added
    run_max, run_total, run_accum = (new_max, run_total, run_accum)
    summed = run_accum / run_total[:, :, None]
    attended = (
        jnp.transpose(summed, (1, 0, 2)).reshape(tok_rows, heads_here * HD).astype(jnp.bfloat16)
    )
    projected = jnp.dot(
        attended,
        lax.all_gather(out_weight, "seq", axis=1, tiled=True),
        preferred_element_type=jnp.float32,
    )
    shared = lax.psum_scatter(
        projected.astype(jnp.bfloat16), "head", scatter_dimension=1, tiled=True
    ).astype(jnp.float32)
    my_step = jnp.sum(jnp.where(group_ids == my_span, step_index, 0))
    step_ids = jnp.arange(gate_table.shape[0], dtype=jnp.int32)
    gate_row = jnp.sum(jnp.where((step_ids == my_step)[:, None], gate_table, 0.0), axis=0)
    return (gate_row[None, :] * shared).astype(jnp.bfloat16)


def solution(mesh):
    in_specs = (
        P(("streams", "span", "seq"), "head"),
        P(("streams", "span", "seq"), "head"),
        P(("streams", "span", "seq"), "head"),
        P("head", "seq"),
        P(None, "head"),
        P("streams"),
        P("streams", None),
    )
    out_specs = P(("streams", "span", "seq"), "head")
    return jax.shard_map(
        on_device, mesh=mesh, in_specs=in_specs, out_specs=out_specs, check_vma=False
    )
```

profile of v0, /device:TPU:0, one launch (start us, length us, event | category | flops | bytes accessed | tf_op | source)
XLA Modules:
  0.0 153.1 jit_solution(9862988004682840681)
XLA Ops:
  6.5 0.0 all-gather.6.cloned.1.call-start
  6.5 0.7 all-gather.6.cloned.1.call-update
  7.3 0.0 all-gather.4.cloned.1.call-start
  7.3 1.9 %copy.16 = bf16[256,640]{0,1:T(8,128)(2,1)} copy(bf16[256,640]{1,0:T(8,128)(2,1)} %param.8) | data formatting | bytes 655360 | tf_op args[1]
  9.2 0.0 all-gather.4.cloned.1.call-update
  9.2 0.0 all-gather.8.cloned.1.call-start
  9.2 0.7 all-gather.8.cloned.1.call-update
  9.9 0.0 reduce-scatter.2.cloned.1.call-start
  10.0 1.1 copy.15
  11.2 0.8 select_reduce_fusion.2
  11.9 0.1 select_reduce_fusion.1
  12.0 33.6 %all-gather.6.cloned.1.call-done = bf16[2048,640]{1,0:T(8,128)(2,1)} async-done(((bf16[256,640]{1,0:T(8,128)(2,1)}), bf16[2048,640]{1,0:T(8,128)(2,1)}) %all-gather.6.cloned.1.call-update) | async-done | bytes 2621456 | tf_op jit(solution)/shard_map/all_gather | solution.py:23
  45.6 3.0 %copy.19 = bf16[2048,640]{0,1:T(8,128)(2,1)S(1)} copy(bf16[2048,640]{1,0:T(8,128)(2,1)} %all-gather.6.cloned.1.call-done) | data formatting | bytes 5242880 | tf_op jit(solution)/shard_map/all_gather | solution.py:23
  48.6 32.5 %all-gather.4.cloned.1.call-done = bf16[2048,640]{0,1:T(8,128)(2,1)} async-done(((bf16[256,640]{0,1:T(8,128)(2,1)}), bf16[2048,640]{0,1:T(8,128)(2,1)}) %all-gather.4.cloned.1.call-update) | async-done | bytes 2621456 | tf_op jit(solution)/shard_map/all_gather | solution.py:22
  81.1 3.7 %fusion = (f32[5,256]{1,0:T(8,128)S(1)}, f32[5,256,2048]{2,1,0:T(8,128)S(1)}) fusion(pred[2048]{0:T(1024)(128)(4,1)S(1)} %broadcast_compare_fusion, bf16[256,5,128]{0,2,1:T(8,128)(2,1)S(1)} %bitcast.18, bf16[2048,5,128]{0,2,1:T(8,128)(2,1)} %bitcast.16), kind=kOutput, calls=%fused_computation.2 | convolution fusion | flops 678951680 | bytes 13442048 | tf_op jit(solution)/shard_map/thd,khd->htk/dot_general | solution.py:31
  84.8 2.6 %fusion.1 = f32[5,256]{1,0:T(8,128)S(1)} fusion(f32[5,256,2048]{2,1,0:T(8,128)S(1)} %get-tuple-element.6, f32[5,256]{1,0:T(8,128)S(1)} %broadcast_maximum_fusion, pred[2048]{0:T(1024)(128)(4,1)S(1)} %broadcast_compare_fusion), kind=kLoop, calls=%fused_computation.3 | loop fusion | flops 13105920 | bytes 10498048 | tf_op jit(solution)/shard_map/reduce_sum | solution.py:42
  87.3 3.3 %fusion.12 = bf16[256,5,128]{0,2,1:T(8,128)(2,1)S(1)} fusion(bf16[2048,5,128]{0,2,1:T(8,128)(2,1)S(1)} %bitcast.17, f32[5,256,2048]{2,1,0:T(8,128)S(1)} %get-tuple-element.6, f32[5,256]{1,0:T(8,128)S(1)} %broadcast_maximum_fusion, pred[2048]{0:T(1024)(128)(4,1)S(1)} %broadcast_compare_fusion, f32[256,5]{0,1:T(8,128)S(1)} %bitcast.20), kind=kOutput, calls=%fused_computation.11 | convolution fusion | flops 684523520 | bytes 13447168 | tf_op jit(solution)/shard_map/htk,khd->htd/dot_general | solution.py:43
  90.6 7.7 %all-gather.8.cloned.1.call-done = bf16[640,5120]{1,0:T(8,128)(2,1)} async-done(((bf16[640,2560]{1,0:T(8,128)(2,1)}), bf16[640,5120]{1,0:T(8,128)(2,1)}) %all-gather.8.cloned.1.call-update) | async-done | bytes 6553616 | tf_op jit(solution)/shard_map/all_gather | solution.py:57
  98.4 0.0 copy-start.1
  98.4 0.0 copy-start
  98.4 6.7 %convolution_convert_fusion = bf16[256,5120]{1,0:T(8,128)(2,1)} fusion(bf16[256,640]{0,1:T(8,128)(2,1)S(1)} %bitcast.19, bf16[640,5120]{1,0:T(8,128)(2,1)} %all-gather.8.cloned.1.call-done), kind=kOutput, calls=%fused_computation.5 | convolution fusion | flops 1679032320 | bytes 9502720 | tf_op jit(solution)/shard_map/dot_general | solution.py:55
  105.0 0.0 reduce-scatter.2.cloned.1.call-update
  105.1 0.0 copy-done.1
  105.1 0.6 select_reduce_fusion.3
  105.7 0.6 iota_compare_fusion.2
  106.4 0.0 copy-done
  106.4 0.1 select_reduce_fusion
  106.5 37.5 %reduce-scatter.2.cloned.1.call-done = bf16[256,2560]{1,0:T(8,128)(2,1)} async-done(((bf16[256,5120]{1,0:T(8,128)(2,1)}), bf16[256,2560]{1,0:T(8,128)(2,1)}) %reduce-scatter.2.cloned.1.call-update) | async-done | bytes 1310736 | tf_op jit(solution)/shard_map/reduce_scatter | solution.py:60
  144.0 2.6 %multiply_convert_fusion = bf16[256,2560]{1,0:T(8,128)(2,1)} fusion(bf16[256,2560]{1,0:T(8,128)(2,1)} %reduce-scatter.2.cloned.1.call-done, f32[2560]{0:T(1024)S(1)} %select_reduce_fusion), kind=kLoop, calls=%fused_computation.8 | loop fusion | flops 1966080 | bytes 2631680 | tf_op jit(solution)/shard_map/convert_element_type | solution.py:66
  (4 shorter events, 0.0 us)
Async XLA Ops:
  6.5 39.1 %all-gather.6.cloned.1.call-start = ((), (), s32[]{:S(2)}) async-start(), calls=%async_computation.2 | async-start | bytes 2949120 | tf_op jit(solution)/shard_map/all_gather | solution.py:23
  7.3 73.8 %all-gather.4.cloned.1.call-start = ((), (), s32[]{:S(2)}) async-start(), calls=%async_computation.1 | async-start | bytes 2949120 | tf_op jit(solution)/shard_map/all_gather | solution.py:22
  9.2 89.2 %all-gather.8.cloned.1.call-start = ((), (), s32[]{:S(2)}) async-start(), calls=%async_computation.3 | async-start | bytes 9830400 | tf_op jit(solution)/shard_map/all_gather | solution.py:57
  9.9 134.1 %reduce-scatter.2.cloned.1.call-start = ((), (), s32[]{:S(2)}) async-start(), calls=%async_computation.4 | async-start | bytes 3932160 | tf_op jit(solution)/shard_map/reduce_scatter | solution.py:60
  98.4 6.7 %copy-start.1 = (s32[4]{0:T(128)S(1)}, s32[4]{0:T(128)}, u32[]{:S(2)}) copy-start(s32[4]{0:T(128)} %param.12) | copy-start | bytes 52
  98.4 8.0 %copy-start = (f32[4,2560]{1,0:T(4,128)S(1)}, f32[4,2560]{1,0:T(4,128)}, u32[]{:S(2)}) copy-start(f32[4,2560]{1,0:T(4,128)} %param.11) | copy-start | bytes 122884
Sparse Core Ops, SparseCore 0:
  9.0 36.5 all-gather.5
  47.2 33.8 all-gather.3
  82.6 15.6 all-gather.7
  105.2 38.7 reduce-scatter.1
where the time goes:
time: 153 us
  waiting for transfers between devices  113 us (74%)
  matrix products  13.6 us (9%)
  between operations  13.2 us (9%)
  other arithmetic  7.42 us (5%)
  local copies, waits for them, and re-layouts  6.01 us (4%)
    reduce_scatter x1, waiting for transfers between devices, on_device(): lax.psum_scatter(projected.astype(jnp.bfloat16), 'head', scatter_dimensio...  37.5 us
    all_gather x1, waiting for transfers between devices, on_device(): value_part = lax.all_gather(value_rows, ('span', 'seq'), axis=0, tiled=True)  33.6 us
    all_gather x1, waiting for transfers between devices, on_device(): key_part = lax.all_gather(key_rows, ('span', 'seq'), axis=0, tiled=True)  32.5 us
    all_gather x1, waiting for transfers between devices, on_device(): lax.all_gather(out_weight, 'seq', axis=1, tiled=True)  7.72 us
    dot_general x1, matrix products, on_device(): jnp.dot(attended, lax.all_gather(out_weight, 'seq', axis=1, tiled=True),...  6.68 us
    dot_general x1, matrix products, on_device(): jnp.einsum('thd,khd->htk', query_three, key_part.reshape(piece_rows, head...  3.67 us
    dot_general x1, matrix products, on_device(): jnp.einsum('htk,khd->htd', probs.astype(jnp.bfloat16), value_part.reshape...  3.29 us
  transfers between devices with their start and end apart: 4, of which 4 were waited for; matrix products, arithmetic and copies ran while one was open for 12% of the time, Pallas kernels for 0%

commit v1 on v0

--- a/solution.py
+++ b/solution.py
@@ -19,8 +19,15 @@
     query_three = query_rows.reshape(tok_rows, heads_here, HD)
     score_scale = 1.0 / math.sqrt(HD)
     run_max = jnp.full((heads_here, tok_rows), NEG_FLOOR, jnp.float32)
-    key_part = lax.all_gather(key_rows, ("span", "seq"), axis=0, tiled=True)
-    value_part = lax.all_gather(value_rows, ("span", "seq"), axis=0, tiled=True)
+
+    def supply_all_the_lines(s0, z):
+        return jnp.split(
+            lax.all_gather(jnp.concatenate([s0, z], axis=1), ("span", "seq"), axis=0, tiled=True),
+            [s0.shape[1]],
+            axis=1,
+        )
+
+    key_part, value_part = supply_all_the_lines(key_rows, value_rows)
     piece_rows = key_part.shape[0]
     key_group = jnp.arange(piece_rows, dtype=jnp.int32) // span_tok
     visible = (

time: 153 us -> 141 us (0.922)
  waiting for transfers between devices: 113 us -> 101 us
    all_gather x2 -> x1, waiting for transfers between devices: 66.1 us -> 58.1 us  [supply_all_the_lines(): lax.all_gather(jnp.concatenate([s0, z], axis=1), ('span', 'seq'), axis=0,...]
    split x0 -> x1, local copies, waits for them, and re-layouts: none -> 3.2 us  [supply_all_the_lines(): jnp.split(lax.all_gather(jnp.concatenate([s0, z], axis=1), ('span', 'seq'...]
    all_gather x1, waiting for transfers between devices: 7.72 us -> 4.61 us  [on_device(): lax.all_gather(out_weight, 'seq', axis=1, tiled=True)]
    all_gather x1 -> x0, local copies, waits for them, and re-layouts: 2.99 us -> none  [on_device(): value_part = lax.all_gather(value_rows, ('span', 'seq'), axis=0, tiled=True)]
  transfers between devices with their start and end apart: 4 -> 3, of which waited for: 4 -> 3; matrix products, arithmetic and copies ran while one was open for 12% -> 10% of each run, Pallas kernels for 0% -> 0%
where the time goes in v1:
time: 141 us
  waiting for transfers between devices  101 us (72%)
  between operations  13.2 us (9%)
  matrix products  12.5 us (9%)
  other arithmetic  8.25 us (6%)
  local copies, waits for them, and re-layouts  5.73 us (4%)
    all_gather x1, waiting for transfers between devices, supply_all_the_lines(): lax.all_gather(jnp.concatenate([s0, z], axis=1), ('span', 'seq'), axis=0,...  58.1 us
    reduce_scatter x1, waiting for transfers between devices, on_device(): lax.psum_scatter(projected.astype(jnp.bfloat16), 'head', scatter_dimensio...  37.5 us
    dot_general x1, matrix products, on_device(): jnp.dot(attended, lax.all_gather(out_weight, 'seq', axis=1, tiled=True),...  6.68 us
    all_gather x1, waiting for transfers between devices, on_device(): lax.all_gather(out_weight, 'seq', axis=1, tiled=True)  4.61 us
    split x1, local copies, waits for them, and re-layouts, supply_all_the_lines(): jnp.split(lax.all_gather(jnp.concatenate([s0, z], axis=1), ('span', 'seq'...  3.2 us
    reduce_sum x1, other arithmetic, on_device(): run_total = jnp.sum(probs, axis=2)  3.2 us
    dot_general x1, matrix products, on_device(): jnp.einsum('thd,khd->htk', query_three, key_part.reshape(piece_rows, head...  3.02 us
    dot_general x1, matrix products, on_device(): jnp.einsum('htk,khd->htd', probs.astype(jnp.bfloat16), value_part.reshape...  2.84 us
  transfers between devices with their start and end apart: 3, of which 3 were waited for; matrix products, arithmetic and copies ran while one was open for 10% of the time, Pallas kernels for 0%

profile of v1, /device:TPU:0, one launch (start us, length us, event | category | flops | bytes accessed | tf_op | source)
XLA Modules:
  0.0 140.8 jit_solution(3415100250800236020)
XLA Ops:
  6.5 0.0 copy-start
  6.5 0.0 copy-start.2
  6.5 0.0 all-gather.3.cloned.1.call-start
  6.5 1.2 copy.18
  7.7 1.1 copy.17
  8.9 0.9 pad_maximum_fusion
  9.8 0.0 all-gather.3.cloned.1.call-update
  9.8 0.0 all-gather.5.cloned.1.call-start
  9.8 0.7 all-gather.5.cloned.1.call-update
  10.5 0.0 reduce-scatter.2.cloned.1.call-start
  10.6 0.0 copy-done
  10.6 0.2 copy.19
  10.8 0.0 copy-done.2
  10.8 0.1 select_reduce_fusion.2
  10.9 0.1 select_reduce_fusion.1
  11.0 58.1 %all-gather.3.cloned.1.call-done = bf16[2048,1280]{0,1:T(8,128)(2,1)} async-done(((bf16[256,1280]{0,1:T(8,128)(2,1)}), bf16[2048,1280]{0,1:T(8,128)(2,1)}) %all-gather.3.cloned.1.call-update) | async-done | bytes 5242896 | tf_op jit(solution)/shard_map/all_gather | solution.py:25
  69.1 3.2 %fusion.23 = (bf16[2048,640]{0,1:T(8,128)(2,1)S(1)}, bf16[2048,640]{0,1:T(8,128)(2,1)S(1)}) fusion(bf16[2048,1280]{0,1:T(8,128)(2,1)} %all-gather.3.cloned.1.call-done), kind=kLoop, calls=%fused_computation.35 | loop fusion | bytes 10485760 | tf_op jit(solution)/shard_map/split | solution.py:24
  72.4 3.0 %bitcast_reduce_fusion = (f32[5,256]{1,0:T(8,128)S(1)}, f32[5,2048,256]{2,1,0:T(8,128)S(1)}) fusion(pred[2048]{0:T(1024)(128)(4,1)S(1)} %broadcast_compare_fusion, bf16[2048,5,128]{0,2,1:T(8,128)(2,1)S(1)} %bitcast.34, bf16[256,5,128]{0,2,1:T(8,128)(2,1)S(1)} %bitcast.36), kind=kOutput, calls=%fused_computation.1 | convolution fusion | flops 678951680 | bytes 13442048 | tf_op jit(solution)/shard_map/thd,khd->htk/dot_general | solution.py:38
  75.4 3.2 %fusion.2 = f32[5,256]{1,0:T(8,128)S(1)} fusion(f32[5,2048,256]{2,1,0:T(8,128)S(1)} %get-tuple-element.8, f32[5,256]{1,0:T(8,128)S(1)} %broadcast_maximum_fusion, pred[2048]{0:T(1024)(128)(4,1)S(1)} %broadcast_compare_fusion), kind=kLoop, calls=%fused_computation.5 | loop fusion | flops 13105920 | bytes 10498048 | tf_op jit(solution)/shard_map/reduce_sum | solution.py:49
  78.6 2.8 %fusion.14 = bf16[256,5,128]{0,2,1:T(8,128)(2,1)S(1)} fusion(bf16[2048,5,128]{0,2,1:T(8,128)(2,1)S(1)} %bitcast.35, f32[5,2048,256]{2,1,0:T(8,128)S(1)} %get-tuple-element.8, f32[5,256]{1,0:T(8,128)S(1)} %broadcast_maximum_fusion, pred[2048]{0:T(1024)(128)(4,1)S(1)} %broadcast_compare_fusion, f32[256,5]{0,1:T(8,128)S(1)} %bitcast.38), kind=kOutput, calls=%fused_computation.14 | convolution fusion | flops 684523520 | bytes 13447168 | tf_op jit(solution)/shard_map/htk,khd->htd/dot_general | solution.py:50
  81.4 4.6 %all-gather.5.cloned.1.call-done = bf16[640,5120]{1,0:T(8,128)(2,1)} async-done(((bf16[640,2560]{1,0:T(8,128)(2,1)}), bf16[640,5120]{1,0:T(8,128)(2,1)}) %all-gather.5.cloned.1.call-update) | async-done | bytes 6553616 | tf_op jit(solution)/shard_map/all_gather | solution.py:64
  86.1 0.0 copy-start.3
  86.1 0.0 copy-start.1
  86.1 6.7 %convolution_convert_fusion = bf16[256,5120]{1,0:T(8,128)(2,1)} fusion(bf16[256,640]{0,1:T(8,128)(2,1)S(1)} %bitcast.37, bf16[640,5120]{1,0:T(8,128)(2,1)} %all-gather.5.cloned.1.call-done), kind=kOutput, calls=%fused_computation.7 | convolution fusion | flops 1679032320 | bytes 9502720 | tf_op jit(solution)/shard_map/dot_general | solution.py:62
  92.7 0.0 reduce-scatter.2.cloned.1.call-update
  92.8 0.0 copy-done.3
  92.8 0.6 select_reduce_fusion.3
  93.4 0.6 iota_compare_fusion.2
  94.1 0.0 copy-done.1
  94.1 0.1 select_reduce_fusion
  94.2 37.5 %reduce-scatter.2.cloned.1.call-done = bf16[256,2560]{1,0:T(8,128)(2,1)} async-done(((bf16[256,5120]{1,0:T(8,128)(2,1)}), bf16[256,2560]{1,0:T(8,128)(2,1)}) %reduce-scatter.2.cloned.1.call-update) | async-done | bytes 1310736 | tf_op jit(solution)/shard_map/reduce_scatter | solution.py:67
  131.7 2.6 %multiply_convert_fusion = bf16[256,2560]{1,0:T(8,128)(2,1)} fusion(bf16[256,2560]{1,0:T(8,128)(2,1)} %reduce-scatter.2.cloned.1.call-done, f32[2560]{0:T(1024)S(1)} %select_reduce_fusion), kind=kLoop, calls=%fused_computation.11 | loop fusion | flops 1966080 | bytes 2631680 | tf_op jit(solution)/shard_map/convert_element_type | solution.py:73
  (4 shorter events, 0.0 us)
Async XLA Ops:
  6.5 4.1 %copy-start = (bf16[256,640]{1,0:T(8,128)(2,1)S(1)}, bf16[256,640]{1,0:T(8,128)(2,1)}, u32[]{:S(2)}) copy-start(bf16[256,640]{1,0:T(8,128)(2,1)} %param.7) | copy-start | bytes 983044
  6.5 4.3 %copy-start.2 = (s32[4,4]{1,0:T(4,128)S(1)}, s32[4,4]{1,0:T(4,128)}, u32[]{:S(2)}) copy-start(s32[4,4]{1,0:T(4,128)} %param.13) | copy-start | bytes 196
  6.5 62.6 %all-gather.3.cloned.1.call-start = ((), (), s32[]{:S(2)}) async-start(), calls=%async_computation.1 | async-start | bytes 5898240 | tf_op jit(solution)/shard_map/all_gather | solution.py:25
  9.8 76.3 %all-gather.5.cloned.1.call-start = ((), (), s32[]{:S(2)}) async-start(), calls=%async_computation.2 | async-start | bytes 9830400 | tf_op jit(solution)/shard_map/all_gather | solution.py:64
  10.5 121.1 %reduce-scatter.2.cloned.1.call-start = ((), (), s32[]{:S(2)}) async-start(), calls=%async_computation.3 | async-start | bytes 3932160 | tf_op jit(solution)/shard_map/reduce_scatter | solution.py:67
  86.1 6.7 %copy-start.3 = (s32[4]{0:T(128)S(1)}, s32[4]{0:T(128)}, u32[]{:S(2)}) copy-start(s32[4]{0:T(128)} %param.12) | copy-start | bytes 52
  86.1 8.0 %copy-start.1 = (f32[4,2560]{1,0:T(4,128)S(1)}, f32[4,2560]{1,0:T(4,128)}, u32[]{:S(2)}) copy-start(f32[4,2560]{1,0:T(4,128)} %param.11) | copy-start | bytes 122884
Sparse Core Ops, SparseCore 0:
  9.9 59.1 all-gather.2
  70.7 15.3 all-gather.4
  92.9 38.7 reduce-scatter.1
